TPU v7x, 32 devices: a whole 2x2x4 slice. The times are simulated.
32 devices in a mesh: clip: 8 (over z, core), frame: 4 (over y, x).
Axes of the slice: x: 2, y: 2, z: 4, core: 2. Of those that a mesh axis runs over, the one named last changes fastest.
Arguments:
- block_input: bfloat16 [16, 16, 64, 1152], P('clip', 'frame'), may hold values from -6 to 6
- modulation: bfloat16 [16, 6912], P('clip'), may hold values from -4 to 4
- frame_counts: int32 [16], P('clip'), may hold values from 8 to 16, as said below
- qkv_weight: bfloat16 [1152, 3456], replicated, may hold values from -0.1875 to 0.1875
- qv_bias: bfloat16 [2304], replicated, may hold values from -3 to 3
- out_weight: bfloat16 [1152, 1152], replicated, may hold values from -0.375 to 0.375
- out_bias: bfloat16 [1152], replicated, may hold values from -3 to 3
- fc1_weight: bfloat16 [1152, 4608], replicated, may hold values from -0.1875 to 0.1875
- fc1_bias: bfloat16 [4608], replicated, may hold values from -3 to 3
- fc2_weight: bfloat16 [4608, 1152], replicated, may hold values from -0.09375 to 0.09375
- fc2_bias: bfloat16 [1152], replicated, may hold values from -3 to 3
- out_cotangent: bfloat16 [16, 16, 64, 1152], P('clip', 'frame'), may hold values from -6 to 6
Outputs:
- block_output: bfloat16 [16, 16, 64, 1152], P('clip', 'frame')
- input_grad: bfloat16 [16, 16, 64, 1152], P('clip', 'frame')
- modulation_grad: float32 [16, 6912], P('clip', 'frame')
- qkv_weight_grad: float32 [1152, 3456], P('clip', 'frame')
- qv_bias_grad: float32 [2304], P('frame')
- out_weight_grad: float32 [1152, 1152], P('clip', 'frame')
- out_bias_grad: float32 [1152], P('frame')
- fc1_weight_grad: float32 [1152, 4608], P('clip', 'frame')
- fc1_bias_grad: float32 [4608], P('frame')
- fc2_weight_grad: float32 [4608, 1152], P('clip', 'frame')
- fc2_bias_grad: float32 [1152], P('frame')
Inputs may be any that keep to these rules, and one draw needn't show every extreme that they name: `frame_counts`: each clip holds 8 to 16 frames in its leading slots; some clip holds 16 and some other clip 16 // 2.
All inputs are finite; a program needn't handle non-finite values.
Results may differ from a plain program's by a relative error of at most 0.013.
The roundings to bfloat16 on the way count: a program that leaves them out, or rounds other values in their place, can miss the bound.
Values may be sent and summed in bfloat16 or wider, within the bound.
A program may use at most 256 MiB of HBM per device.

v0:
```python
import functools

import jax
import jax.numpy as jnp
from jax import lax
from jax.experimental import pallas as pl
from jax.experimental.pallas import tpu as pltpu
from jax.sharding import PartitionSpec as P

HEADS = 16


EPSILON = 1e-06
NEGATIVE = -1e30


def normalize(values):
    centred = values - jnp.mean(values, axis=-1, keepdims=True)
    variance = jnp.mean(centred * centred, axis=-1, keepdims=True)
    return centred * lax.rsqrt(variance + EPSILON)


def modulate(values, shift_term, scale_term):
    return normalize(values) * (1.0 + scale_term) + shift_term


def gelu_tanh(inputs):
    return jax.nn.gelu(inputs, approximate=True)


def contract_rows(left, right):
    return lax.dot_general(
        left, right, (((0,), (0,)), ((), ())), preferred_element_type=jnp.float32
    )


def contract_cols(left, right):
    return lax.dot_general(
        left, right, (((1,), (1,)), ((), ())), preferred_element_type=jnp.float32
    )


def on_device(
    block_input,
    modulation,
    frame_counts,
    qkv_weight,
    qv_bias,
    out_weight,
    out_bias,
    fc1_weight,
    fc1_bias,
    fc2_weight,
    fc2_bias,
    out_cotangent,
):
    swapped = lax.all_to_all(block_input, "frame", split_axis=2, concat_axis=1, tiled=True)
    clip_count, frames, patches, model_width = swapped.shape
    head_width = model_width // HEADS
    row_count = clip_count * frames * patches
    factor = head_width ** (-0.5)
    frame_valid = (jnp.arange(frames)[None, :] < frame_counts[:, None]).astype(jnp.float32)
    valid_rows = frame_valid[:, :, None, None]
    key_valid = frame_valid[:, None, None, None, :] > 0.5
    modulators = modulation.astype(jnp.float32).reshape(clip_count, 6, model_width)[
        :, :, None, None, :
    ]
    shift_one = modulators[:, 0]
    scale_one = modulators[:, 1]
    gate_one = modulators[:, 2]
    shift_two = modulators[:, 3]
    scale_two = modulators[:, 4]
    gate_two = modulators[:, 5]
    residual = swapped.astype(jnp.float32)
    normed_full, modulate_back_one = jax.vjp(modulate, residual, shift_one, scale_one)
    normed_one = normed_full.astype(jnp.bfloat16).reshape(row_count, model_width)
    bias_full = jnp.concatenate(
        [qv_bias[:model_width], jnp.zeros((model_width,), jnp.bfloat16), qv_bias[model_width:]]
    ).astype(jnp.float32)
    projected = (
        jnp.dot(normed_one, qkv_weight, preferred_element_type=jnp.float32) + bias_full
    ).astype(jnp.bfloat16)
    shaped = projected.reshape(clip_count, frames, patches, 3, HEADS, head_width)
    queries = shaped[:, :, :, 0]
    keys_all = shaped[:, :, :, 1]
    values_all = shaped[:, :, :, 2]
    scores = (
        jnp.einsum("cfphd,cgphd->cphfg", queries, keys_all, preferred_element_type=jnp.float32)
        * factor
    )
    scores = jnp.where(key_valid, scores, NEGATIVE)
    row_peak = jnp.max(scores, axis=-1, keepdims=True)
    exponent = jnp.exp(scores - row_peak)
    attention_weights = exponent / jnp.sum(exponent, axis=-1, keepdims=True)
    weights_low = attention_weights.astype(jnp.bfloat16)
    context = jnp.einsum(
        "cphfg,cgphd->cfphd", weights_low, values_all, preferred_element_type=jnp.float32
    )
    context_low = context.astype(jnp.bfloat16).reshape(row_count, model_width)
    attended = jnp.dot(
        context_low, out_weight, preferred_element_type=jnp.float32
    ) + out_bias.astype(jnp.float32)
    attended = attended.reshape(clip_count, frames, patches, model_width)
    middle = residual + gate_one * attended
    normed_mid, modulate_back_two = jax.vjp(modulate, middle, shift_two, scale_two)
    normed_two = normed_mid.astype(jnp.bfloat16).reshape(row_count, model_width)
    hidden = jnp.dot(normed_two, fc1_weight, preferred_element_type=jnp.float32) + fc1_bias.astype(
        jnp.float32
    )
    activated_full, gelu_back = jax.vjp(gelu_tanh, hidden)
    activated = activated_full.astype(jnp.bfloat16)
    branch_two = jnp.dot(
        activated, fc2_weight, preferred_element_type=jnp.float32
    ) + fc2_bias.astype(jnp.float32)
    branch_two = branch_two.reshape(clip_count, frames, patches, model_width)
    result = valid_rows * (middle + gate_two * branch_two)
    block_output = lax.all_to_all(
        result.astype(jnp.bfloat16), "frame", split_axis=1, concat_axis=2, tiled=True
    )
    cotangent = lax.all_to_all(
        out_cotangent, "frame", split_axis=2, concat_axis=1, tiled=True
    ).astype(jnp.float32)
    d_result = valid_rows * cotangent
    d_gate_two = jnp.sum(d_result * branch_two, axis=(1, 2))
    d_branch = (d_result * gate_two).astype(jnp.bfloat16).reshape(row_count, model_width)
    d_fc2_bias = jnp.sum(d_branch.astype(jnp.float32), axis=0)
    d_fc2_weight = contract_rows(activated, d_branch)
    d_activated = contract_cols(d_branch, fc2_weight)
    d_hidden = gelu_back(d_activated)[0].astype(jnp.bfloat16)
    d_fc1_bias = jnp.sum(d_hidden.astype(jnp.float32), axis=0)
    d_fc1_weight = contract_rows(normed_two, d_hidden)
    d_normed_two = contract_cols(d_hidden, fc1_weight).reshape(
        clip_count, frames, patches, model_width
    )
    d_middle_norm, d_shift_two, d_scale_two = modulate_back_two(d_normed_two)
    d_middle = d_result + d_middle_norm
    d_gate_one = jnp.sum(d_middle * attended, axis=(1, 2))
    d_attended = (d_middle * gate_one).astype(jnp.bfloat16).reshape(row_count, model_width)
    d_out_bias = jnp.sum(d_attended.astype(jnp.float32), axis=0)
    d_out_weight = contract_rows(context_low, d_attended)
    d_context = contract_cols(d_attended, out_weight).astype(jnp.bfloat16)
    d_context = d_context.reshape(clip_count, frames, patches, HEADS, head_width)
    d_weights = jnp.einsum(
        "cfphd,cgphd->cphfg", d_context, values_all, preferred_element_type=jnp.float32
    )
    d_values = jnp.einsum(
        "cphfg,cfphd->cgphd", weights_low, d_context, preferred_element_type=jnp.float32
    )
    d_scores = attention_weights * (
        d_weights - jnp.sum(attention_weights * d_weights, axis=-1, keepdims=True)
    )
    d_scores = d_scores.astype(jnp.bfloat16)
    d_queries = (
        jnp.einsum("cphfg,cgphd->cfphd", d_scores, keys_all, preferred_element_type=jnp.float32)
        * factor
    )
    d_keys = (
        jnp.einsum("cphfg,cfphd->cgphd", d_scores, queries, preferred_element_type=jnp.float32)
        * factor
    )
    d_projected = (
        jnp.stack([d_queries, d_keys, d_values], axis=3)
        .astype(jnp.bfloat16)
        .reshape(row_count, 3 * model_width)
    )
    column_sums = jnp.sum(d_projected.astype(jnp.float32), axis=0)
    d_qv_bias = jnp.concatenate([column_sums[:model_width], column_sums[2 * model_width :]])
    d_qkv_weight = contract_rows(normed_one, d_projected)
    d_normed_one = contract_cols(d_projected, qkv_weight).reshape(
        clip_count, frames, patches, model_width
    )
    d_residual, d_shift_one, d_scale_one = modulate_back_one(d_normed_one)
    d_input = d_middle + d_residual
    input_grad = lax.all_to_all(
        d_input.astype(jnp.bfloat16), "frame", split_axis=1, concat_axis=2, tiled=True
    )
    d_modulation = jnp.stack(
        [
            d_shift_one.reshape(clip_count, model_width),
            d_scale_one.reshape(clip_count, model_width),
            d_gate_one,
            d_shift_two.reshape(clip_count, model_width),
            d_scale_two.reshape(clip_count, model_width),
            d_gate_two,
        ],
        axis=1,
    ).reshape(clip_count, 6 * model_width)
    every_part = (
        lax.psum_scatter(d_qkv_weight, "frame", scatter_dimension=1, tiled=True),
        lax.psum_scatter(d_out_weight, "frame", scatter_dimension=1, tiled=True),
        lax.psum_scatter(d_fc1_weight, "frame", scatter_dimension=1, tiled=True),
        lax.psum_scatter(d_fc2_weight, "frame", scatter_dimension=1, tiled=True),
        lax.psum_scatter(d_modulation, "frame", scatter_dimension=1, tiled=True),
        lax.psum_scatter(d_qv_bias, "frame", scatter_dimension=0, tiled=True),
        lax.psum_scatter(d_out_bias, "frame", scatter_dimension=0, tiled=True),
        lax.psum_scatter(d_fc1_bias, "frame", scatter_dimension=0, tiled=True),
        lax.psum_scatter(d_fc2_bias, "frame", scatter_dimension=0, tiled=True),
    )
    every_mat = (
        lax.psum_scatter(every_part[0], "clip", scatter_dimension=0, tiled=True),
        lax.psum_scatter(every_part[1], "clip", scatter_dimension=0, tiled=True),
        lax.psum_scatter(every_part[2], "clip", scatter_dimension=0, tiled=True),
        lax.psum_scatter(every_part[3], "clip", scatter_dimension=0, tiled=True),
    )
    qkv_grad = every_mat[0]
    out_grad = every_mat[1]
    fc1_grad = every_mat[2]
    fc2_grad = every_mat[3]
    modulation_grad = every_part[4]
    bias_parts = (every_part[5], every_part[6], every_part[7], every_part[8])
    bias_totals = lax.psum((bias_parts[0], bias_parts[1], bias_parts[2], bias_parts[3]), "clip")
    return (
        block_output,
        input_grad,
        modulation_grad,
        qkv_grad,
        bias_totals[0],
        out_grad,
        bias_totals[1],
        fc1_grad,
        bias_totals[2],
        fc2_grad,
        bias_totals[3],
    )


LANES = 128
VMEM_LIMIT = 61 * 1024 * 1024
ROWS_DN = (((0,), (0,)), ((), ()))
COLS_DN = (((1,), (1,)), ((), ()))
F32 = jnp.float32
BF16 = jnp.bfloat16


def mm(left, right):
    return jnp.dot(left, right, preferred_element_type=F32)


def mm_cols(left, right):
    return lax.dot_general(left, right, COLS_DN, preferred_element_type=F32)


def mm_rows(left, right):
    return lax.dot_general(left, right, ROWS_DN, preferred_element_type=F32)


def unit(values):
    centred = values - jnp.mean(values, axis=-1, keepdims=True)
    variance = jnp.mean(centred * centred, axis=-1, keepdims=True)
    inverse = lax.rsqrt(variance + EPSILON)
    return centred * inverse, inverse


def unit_back(unit_values, inverse, grad):
    mean_grad = jnp.mean(grad, axis=-1, keepdims=True)
    mean_dot = jnp.mean(grad * unit_values, axis=-1, keepdims=True)
    return (grad - mean_grad - unit_values * mean_dot) * inverse


def params(**more):
    return pltpu.CompilerParams(vmem_limit_bytes=VMEM_LIMIT, **more)


def cost(flops, moved, transcendentals=0):
    return pl.CostEstimate(flops=int(flops), bytes_accessed=int(moved), transcendentals=int(transcendentals))


def shape(dims, kind):
    return jax.ShapeDtypeStruct(tuple(dims), kind)


def whole(dims, buffers=1):
    zeros = (0,) * len(dims)
    return pl.BlockSpec(tuple(dims), lambda *_: zeros, pipeline_mode=pl.Buffered(buffers))


ANY = pl.BlockSpec(memory_space=pl.ANY)


def head_window(head, width):
    low = head * width
    start = low // LANES * LANES
    size = LANES if low - start + width <= LANES else 2 * LANES
    return low, start, size


def head_mask(head, width):
    low, start, size = head_window(head, width)
    lane = lax.broadcasted_iota(jnp.int32, (1, size), 1) + start
    return jnp.where((lane >= low) & (lane < low + width), 1.0, 0.0).astype(BF16)


class Plan:
    def __init__(self, mesh, x, qkv_weight, fc1_weight):
        self.clip_axis = mesh.shape["clip"]
        self.frame_axis = mesh.shape["frame"]
        self.clips, self.local_frames, self.patches, self.width = x
        self.own_patches = self.patches // self.frame_axis
        self.halves = self.own_patches // 8
        self.frames = self.local_frames * self.frame_axis
        self.ff = fc1_weight[1]
        self.rows = self.clips * self.frames * self.own_patches
        self.clip_rows = self.rows // self.clips
        self.block = self.frames * 8
        self.blocks = self.rows // self.block
        self.piece = self.local_frames * 8
        self.head_width = self.width // HEADS
        self.chunk_dims = (self.clips, self.halves, self.local_frames, 8, self.width)
        self.zs = self.clip_axis // 2

    def row_of(self, clip, half, k):
        return ((clip * self.halves + half) * self.frame_axis + k) * self.piece


def fits(mesh, x, qkv_weight, fc1_weight):
    clip_axis, frame_axis = mesh.shape["clip"], mesh.shape["frame"]
    width, ff = x[3], fc1_weight[1]
    return (
        clip_axis == 8
        and frame_axis == 4
        and x[2] // frame_axis % 8 == 0
        and x[1] * frame_axis * 8 == LANES
        and width == 1152
        and ff == 4 * width
        and qkv_weight[1] == 3 * width
    )


def fold_tile(tile, folds, used):
    rows = tile.shape[0] // folds
    total = tile[:rows]
    for g in range(1, folds):
        total = total + pltpu.roll(tile[g * rows : (g + 1) * rows], g * used, 1)
    return total


MESH = pl.DeviceIdType.MESH


def unit_rows(ref, here):
    return unit(ref[here, :])


class Later:
    def __init__(self, make):
        self.make = make

    def start(self):
        self.make().start()

    def wait(self):
        self.make().wait()

    def wait_recv(self):
        self.make().wait_recv()

    def wait_send(self):
        self.make().wait_send()


REMOTE_SIZES = (4, 4, 8, 1, 4, 4, 4, 4, 1, 1, 4, 2, 2, 1, 1, 1, 1, 1, 1, 1, 1, 1, 2, 2, 2, 2, 2, 2, 2, 2, 1, 4, 4, 2, 2, 3, 4, 4)
(
    R_C2, R_C1, R_C0, R_CO, R_2AX, R_2BY, R_2AY, R_2BX, R_2Z, R_2ZZ, R_1Z, R_1AX, R_1BY, R_1AY, R_1BX, R_1ZZ, R_OAX, R_OBY, R_OAY, R_OBX, R_OZ, R_OZZ, R_0AX, R_0BY, R_0CZ, R_0AY, R_0BX, R_0CX, R_0ABZ, R_0CY, R_0ZZ, R_OUT, R_IN, R_SMX, R_SMY, R_SMC, R_XIN, R_CIN,
) = REMOTE_AT = tuple(sum(REMOTE_SIZES[:i]) for i in range(len(REMOTE_SIZES)))
LOCAL_SIZES = (4, 6, 6, 6, 6, 2, 1, 1, 1, 2, 1, 1, 4, 1, 4)
(
    L_W, L_A, L_B, L_C, L_D, L_S, L_MID, L_ATT, L_PROJ, L_PROBS, L_N1, L_CTX, L_OWN, L_ACT, L_ACTS,
) = LOCAL_AT = tuple(sum(LOCAL_SIZES[:i]) for i in range(len(LOCAL_SIZES)))
CORE, Z0, Z1, X, Y, XY = range(6)


LOAD, RUN, SEND = range(3)
TMP_A, TMP_B, TMP_C, TMP_D, TMP_S = range(5)
(J_C1, J_C2, J_Z0, J_XY1, J_XY2, J_1A, J_1B, J_1XY2, J_2Z, J_CO, J_O1, J_O2, J_OZ, J_C0, J_Q1, J_Q2, J_Q3, J_FIN2, J_FIN1, J_FINO, J_FIN0, J_SM1, J_SM2, J_SM3, J_SM4, J_SM5, J_MD1, J_MD2) = range(28)
(S_1AX, S_1BY, S_1AY, S_1BX, S_2Z, S_0ZZ, S_SMX, S_MDX, S_OUT, S_IN) = range(10)
P_A = tuple((0, k) for k in range(4))
P_B = tuple((1, k) for k in range(4))
P_C = tuple((2, k) for k in range(4))
P_D = tuple((3, k) for k in range(4))
P_E = tuple((4, k) for k in range(4))
P_G = tuple((5, k) for k in range(4))
P_AB = tuple((6, k) for k in range(4))
P_WQ = tuple((7, k) for k in range(8))
P_IN = tuple((9, k) for k in range(3))
P_M1, P_O, P_WO, P_DC, P_PK, P_INE = ((8, k) for k in range(6))
SCHEDULE = {
    P_E[0]: (
        (LOAD, J_C2, 0),
    ),
    P_A[1]: (
        (RUN, J_C2, 0),
        (LOAD, J_C1, 0),
    ),
    P_B[1]: (
        (RUN, J_C1, 0),
    ),
    P_D[1]: (
        (LOAD, J_C2, 1),
    ),
    P_E[1]: (
        (RUN, J_C2, 1),
    ),
    P_A[2]: (
        (LOAD, J_C1, 1),
        (LOAD, J_XY1, 0),
    ),
    P_B[2]: (
        (RUN, J_C1, 1),
    ),
    P_D[2]: (
        (RUN, J_XY1, 0),
    ),
    P_E[2]: (
        (LOAD, J_XY1, 1),
    ),
    P_A[3]: (
        (LOAD, J_C2, 2),
        (RUN, J_XY1, 1),
        (LOAD, J_C1, 2),
    ),
    P_B[3]: (
        (LOAD, J_Z0, 0),
        (RUN, J_C2, 2),
        (LOAD, J_XY2, 0),
    ),
    P_C[3]: (
        (RUN, J_C1, 2),
    ),
    P_D[3]: (
        (RUN, J_Z0, 0),
        (LOAD, J_C2, 3),
    ),
    P_E[3]: (
        (RUN, J_C2, 3),
        (RUN, J_XY2, 0),
    ),
    P_M1: (
        (LOAD, J_C1, 3),
        (LOAD, J_XY1, 2),
    ),
    P_WO: (
        (RUN, J_C1, 3),
        (LOAD, J_XY2, 1),
        (RUN, J_XY1, 2),
    ),
    P_DC: (
        (RUN, J_XY2, 1),
        (LOAD, J_XY1, 3),
    ),
    P_AB[0]: (
        (RUN, J_XY1, 3),
    ),
    P_AB[1]: (
        (LOAD, J_CO, 0),
    ),
    P_AB[2]: (
        (RUN, J_CO, 0),
        (LOAD, J_XY2, 2),
        (RUN, J_XY2, 2),
        (LOAD, J_XY2, 3),
    ),
    P_AB[3]: (
        (RUN, J_XY2, 3),
        (LOAD, J_Z0, 1),
    ),
    P_PK: (
        (RUN, J_Z0, 1),
        (SEND, S_1AX, 0),
    ),
    P_WQ[0]: (
        (LOAD, J_Z0, 2),
    ),
    P_WQ[1]: (
        (RUN, J_Z0, 2),
    ),
    P_WQ[2]: (
        (SEND, S_1BY, 0),
        (SEND, S_2Z, 0),
    ),
    P_WQ[4]: (
        (LOAD, J_Z0, 3),
    ),
    P_WQ[5]: (
        (RUN, J_Z0, 3),
        (SEND, S_1AX, 1),
        (SEND, S_1BY, 1),
    ),
    P_WQ[6]: (
        (LOAD, J_C0, 0),
    ),
    P_WQ[7]: (
        (LOAD, J_O1, 0),
        (RUN, J_O1, 0),
    ),
    P_IN[0]: (
        (LOAD, J_1A, 0),
        (RUN, J_1A, 0),
        (RUN, J_C0, 0),
    ),
    P_IN[1]: (
        (LOAD, J_1B, 0),
    ),
    P_IN[2]: (
        (RUN, J_1B, 0),
        (LOAD, J_C0, 1),
    ),
    P_INE: (
        (RUN, J_C0, 1),
        (SEND, S_SMX, 0),
    ),
    P_G[0]: (
        (LOAD, J_2Z, 0),
        (RUN, J_2Z, 0),
        (LOAD, J_1B, 1),
        (RUN, J_1B, 1),
    ),
    P_G[1]: (
        (SEND, S_1BX, 0),
        (LOAD, J_1A, 1),
    ),
    P_G[2]: (
        (RUN, J_1A, 1),
        (LOAD, J_O2, 0),
        (LOAD, J_SM1, 0),
        (LOAD, J_Q1, 0),
        (RUN, J_Q1, 0),
        (RUN, J_O2, 0),
        (RUN, J_SM1, 0),
        (SEND, S_1AY, 0),
        (LOAD, J_Q1, 1),
        (LOAD, J_SM2, 0),
        (RUN, J_SM2, 0),
        (LOAD, J_SM3, 0),
        (RUN, J_SM3, 0),
        (RUN, J_Q1, 1),
        (LOAD, J_OZ, 0),
    ),
    P_G[3]: (
        (LOAD, J_SM4, 0),
        (RUN, J_OZ, 0),
        (LOAD, J_Q2, 0),
        (RUN, J_SM4, 0),
        (RUN, J_Q2, 0),
        (LOAD, J_1XY2, 0),
    ),
    P_O: (
        (SEND, S_OUT, 3),
        (SEND, S_OUT, 1),
        (SEND, S_OUT, 2),
        (RUN, J_1XY2, 0),
        (LOAD, J_SM5, 0),
        (LOAD, J_Q2, 1),
        (RUN, J_Q2, 1),
        (LOAD, J_FINO, 0),
        (SEND, S_MDX, 0),
        (RUN, J_FINO, 0),
        (LOAD, J_FIN2, 0),
        (LOAD, J_Q3, 0),
        (RUN, J_Q3, 0),
        (LOAD, J_MD1, 0),
        (RUN, J_MD1, 0),
        (RUN, J_SM5, 0),
        (LOAD, J_Q3, 1),
        (RUN, J_FIN2, 0),
        (SEND, S_IN, 3),
        (SEND, S_IN, 1),
        (SEND, S_IN, 2),
        (RUN, J_Q3, 1),
        (SEND, S_0ZZ, 0),
        (LOAD, J_FIN1, 0),
        (RUN, J_FIN1, 0),
        (LOAD, J_MD2, 0),
        (LOAD, J_FIN0, 0),
        (RUN, J_MD2, 0),
        (RUN, J_FIN0, 0),
    ),
}
TMPS = {
    (J_1A, 0): TMP_C,
    (J_1A, 1): TMP_C,
    (J_1B, 0): TMP_C,
    (J_1B, 1): TMP_D,
    (J_1XY2, 0): TMP_D,
    (J_2Z, 0): TMP_C,
    (J_C1, 0): TMP_A,
    (J_C1, 1): TMP_A,
    (J_C1, 2): TMP_A,
    (J_C1, 3): TMP_A,
    (J_C2, 0): TMP_B,
    (J_C2, 1): TMP_B,
    (J_C2, 2): TMP_B,
    (J_C2, 3): TMP_B,
    (J_FIN0, 0): TMP_D,
    (J_FIN1, 0): TMP_D,
    (J_FIN2, 0): TMP_C,
    (J_FINO, 0): TMP_C,
    (J_O1, 0): TMP_C,
    (J_O2, 0): TMP_C,
    (J_OZ, 0): TMP_C,
    (J_Q1, 0): TMP_A,
    (J_Q1, 1): TMP_B,
    (J_Q2, 0): TMP_C,
    (J_Q2, 1): TMP_D,
    (J_Q3, 0): TMP_D,
    (J_Q3, 1): TMP_D,
    (J_XY1, 0): TMP_D,
    (J_XY1, 1): TMP_C,
    (J_XY1, 2): TMP_D,
    (J_XY1, 3): TMP_D,
    (J_XY2, 0): TMP_D,
    (J_XY2, 1): TMP_C,
    (J_XY2, 2): TMP_C,
    (J_XY2, 3): TMP_D,
    (J_Z0, 0): TMP_C,
    (J_Z0, 1): TMP_D,
    (J_Z0, 2): TMP_C,
    (J_Z0, 3): TMP_D,
}


def join_heads(width, head_parts, put):
    waiting = {}
    for h in range(HEADS):
        _, start, size = head_window(h, width)
        values = head_parts(h)
        for t in range(size // LANES):
            tiles = [value[:, t * LANES : (t + 1) * LANES] for value in values]
            j = start // LANES + t
            waiting[j] = [a + b for a, b in zip(waiting[j], tiles)] if j in waiting else tiles
        ahead = head_window(h + 1, width)[1] // LANES if h + 1 < HEADS else HEADS * width
        for j in sorted(waiting):
            if j < ahead:
                put(j, waiting.pop(j))


def whole_layer(plan, x, cotangent, modulation, counts, biases, qkv_weight, out_weight, fc1_weight, fc2_weight):
    n, rows, width, ff = plan.frame_axis, plan.rows, plan.width, plan.ff
    own, fl, clips = plan.own_patches, plan.local_frames, plan.clips
    span2, span1 = ff // plan.clip_axis, width // plan.clip_axis
    s1, s0, so = 9 * span1, 7 * span1, 2 * span1 + span1 // 3
    a1, a0 = 640, s0 // 3
    pad2, padq, wq = 384, 896, 3 * width // n
    blocks, block = plan.blocks, plan.block
    factor = plan.head_width ** (-0.5)
    half_rows = 64
    parts_per_clip = plan.clip_rows // half_rows

    def body(*refs):
        refs = list(refs)

        def take(count):
            got = refs[:count]
            del refs[:count]
            return got

        (x_h, cot_h, wqkv_h, wout_h, fc1_h, fc2_h, raw_mod, counts_ref, qv_bias, out_bias, fc1_bias, fc2_bias) = take(12)
        (out_h, in_h) = take(2)
        sum2, sum1, sum0, sumo, small = take(5)
        (rc2, rc1, rc0, rco, r2ax, r2by, r2ay, r2bx, r2z, r2zz) = take(10)
        (r1z, r1ax, r1by, r1ay, r1bx, r1zz) = take(6)
        (roax, roby, roay, robx, roz, rozz) = take(6)
        (r0ax, r0by, r0cz, r0ay, r0bx, r0cx, r0abz, r0cy, r0zz, rsm, rsmc) = take(11)
        (n1_h, ctx_h, proj_h, probs_h, att_h, mid_h, act_h) = take(7)
        (keep2, keep1, keepo, r2, stage, tmp_a, tmp_b, tmp_c, tmp_d, dres, acc, f1, f2, ring, rows_out, sm, sm_b, sm_t, smc) = take(19)
        (xin, cin, mod, bias, allowed, valid) = take(6)
        send_sem, recv_sem, local_sem = take(3)

        frame, clip = lax.axis_index("frame"), lax.axis_index("clip")
        mx, my = frame % 2, frame // 2
        core, z0, z1 = clip % 2, clip // 2 % 2, clip // 4
        partner = (
            ("clip", clip + 1 - 2 * core),
            ("clip", clip + 2 - 4 * z0),
            ("clip", clip + 4 - 8 * z1),
            ("frame", frame + 1 - 2 * mx),
            ("frame", frame + 2 - 4 * my),
            ("frame", n - 1 - frame),
        )

        def remote(name, index, src, dst, bit):
            axis, where = partner[bit]
            at = name + index
            return Later(
                lambda: pltpu.make_async_remote_copy(
                    src_ref=src,
                    dst_ref=dst,
                    send_sem=send_sem.at[at],
                    recv_sem=recv_sem.at[at],
                    device_id={axis: where},
                    device_id_type=MESH,
                )
            )

        def local(name, index, src, dst):
            return Later(lambda: pltpu.make_async_copy(src, dst, local_sem.at[name + index]))

        lo1, hi1 = pl.ds(0, a1), pl.ds(a1, s1 - a1)
        pa, pb, pc, pab, all0 = pl.ds(0, a0), pl.ds(a0, a0), pl.ds(2 * a0, a0), pl.ds(0, 2 * a0), pl.ds(0, s0)
        oa, ob, oab = pl.ds(0, so), pl.ds(so, so), pl.ds(0, 2 * so)
        all1 = pl.ds(0, s1)

        def c2(z):
            return remote(R_C2, z, stage.at[0, :, :, all1], rc2.at[z], CORE)

        def c1(f):
            return remote(R_C1, f, stage.at[1, :, :, all1], rc1.at[f], CORE)

        def c0(j, f):
            return remote(R_C0, 4 * j + f, stage.at[:, f // 2, f % 2, all0], rc0.at[j, :, f // 2, f % 2], CORE)

        def co():
            return remote(R_CO, 0, stage.at[:, :, :, oab], rco, CORE)

        def t2ax(z):
            return remote(R_2AX, z, keep2.at[z // 2, z % 2, :, 1 - mx, lo1], r2ax.at[z], X)

        def t2by(z):
            return remote(R_2BY, z, keep2.at[z // 2, z % 2, 1 - my, :, hi1], r2by.at[z], Y)

        def t2ay(z):
            return remote(R_2AY, z, keep2.at[z // 2, z % 2, 1 - my, mx, lo1], r2ay.at[z], Y)

        def t2bx(z):
            return remote(R_2BX, z, keep2.at[z // 2, z % 2, my, 1 - mx, hi1], r2bx.at[z], X)

        def t2z():
            return remote(R_2Z, 0, r2.at[:, 1 - z0], r2z, Z0)

        def t2zz():
            return remote(R_2ZZ, 0, r2.at[1 - z1, z0], r2zz, Z1)

        def t1z(f):
            return remote(R_1Z, f, keep1.at[f // 2, f % 2, :, 1 - z0], r1z.at[f], Z0)

        def t1ax(y):
            return remote(R_1AX, y, keep1.at[y, 1 - mx, :, z0, lo1], r1ax.at[y], X)

        def t1by(x):
            return remote(R_1BY, x, keep1.at[1 - my, x, :, z0, hi1], r1by.at[x], Y)

        def t1ay():
            return remote(R_1AY, 0, keep1.at[1 - my, mx, :, z0, lo1], r1ay, Y)

        def t1bx():
            return remote(R_1BX, 0, keep1.at[my, 1 - mx, :, z0, hi1], r1bx, X)

        def t1zz():
            return remote(R_1ZZ, 0, keep1.at[my, mx, 1 - z1, z0], r1zz, Z1)

        def toax():
            return remote(R_OAX, 0, keepo.at[:, :, 1 - mx, oa], roax, X)

        def toby():
            return remote(R_OBY, 0, keepo.at[:, 1 - my, :, ob], roby, Y)

        def toay():
            return remote(R_OAY, 0, keepo.at[:, 1 - my, mx, oa], roay, Y)

        def tobx():
            return remote(R_OBX, 0, keepo.at[:, my, 1 - mx, ob], robx, X)

        def toz():
            return remote(R_OZ, 0, keepo.at[1 - z0, my, mx], roz, Z0)

        def tozz():
            there = pl.ds(pl.multiple_of((1 - z1) * so, 16), so)
            return remote(R_OZZ, 0, keepo.at[z0, my, mx, there], rozz, Z1)

        def t0ax(j):
            return remote(R_0AX, j, keep2.at[j, :, :, 1 - mx, pa], r0ax.at[j], X)

        def t0by(j):
            return remote(R_0BY, j, keep2.at[j, :, 1 - my, :, pb], r0by.at[j], Y)

        def t0cz(j):
            return remote(R_0CZ, j, keep2.at[j, 1 - z0, :, :, pc], r0cz.at[j], Z0)

        def t0ay(j):
            return remote(R_0AY, j, keep2.at[j, :, 1 - my, mx, pa], r0ay.at[j], Y)

        def t0bx(j):
            return remote(R_0BX, j, keep2.at[j, :, my, 1 - mx, pb], r0bx.at[j], X)

        def t0cx(j):
            return remote(R_0CX, j, keep2.at[j, z0, :, 1 - mx, pc], r0cx.at[j], X)

        def t0abz(j):
            return remote(R_0ABZ, j, keep2.at[j, 1 - z0, my, mx, pab], r0abz.at[j], Z0)

        def t0cy(j):
            return remote(R_0CY, j, keep2.at[j, z0, 1 - my, mx, pc], r0cy.at[j], Y)

        def t0zz():
            return remote(R_0ZZ, 0, keep2.at[1 - z1, z0, my, mx, all0], r0zz, Z1)

        def row_send(name, k, dst, arriving=False):
            bit = (None, X, Y, XY)[k]
            place = partner[bit][1] if arriving else frame
            src = rows_out if name == R_IN else cin
            return remote(name, k, src.at[k], dst.at[:, :, pl.ds(place * own, own)], bit)

        def row_own(index, src, dst):
            return local(L_OWN, index, src.at[0], dst.at[:, :, pl.ds(frame * own, own)])

        def smx_send():
            return remote(R_SMX, 0, sm.at[0], rsm.at[0, 0], X)

        def smy_send():
            return remote(R_SMY, 0, sm_b.at[0], rsm.at[1, 0], Y)

        def mdx_send():
            return remote(R_SMX, 1, sm.at[pl.ds(1, clips)], rsm.at[0, pl.ds(1, clips)], X)

        def mdy_send():
            return remote(R_SMY, 1, sm_b.at[pl.ds(1, clips)], rsm.at[1, pl.ds(1, clips)], Y)

        def smc_send(i):
            return remote(R_SMC, i, smc.at[i], rsmc.at[i], (CORE, Z0, Z1)[i])

        def add_to(ref, at, other, other_at):
            ref[at] = ref[at] + other[other_at]

        def add_chunks(ref, at, other, other_at, count):
            for i in range(2):
                for k in range(2 if count == 2 else 1):
                    fill = iter((i, k))
                    here = tuple(next(fill) if p is None else p for p in at)
                    fill = iter((i, k))
                    there = tuple(next(fill) if p is None else p for p in other_at)
                    add_to(ref, here, other, there)

        def pump(arrivals, copies, work, sends):
            def load():
                for transfer in arrivals:
                    transfer.wait_recv()
                for copy in copies:
                    copy.start()

            def run():
                for copy in copies:
                    copy.wait()
                work()
                for transfer in sends:
                    transfer.start()

            return load, run

        def job(kind, index, tmps):
            tmp = (tmp_a, tmp_b, tmp_c, tmp_d, None)[tmps]
            sem = (L_A, L_B, L_C, L_D, L_S)[tmps]
            pair = (index // 2, index % 2)
            if kind == J_C1:

                def work():
                    add_chunks(keep1, pair + (None, None), tmp, (None, None, all1), 2)

                return pump([c1(index)], [local(sem, 0, rc1.at[index], tmp.at[:, :, all1])], work, [t1z(index)])
            if kind == J_C2:

                def work():
                    add_chunks(keep2, pair + (None, None, all1), tmp, (None, None, all1), 2)

                sends = [t2ax(index), t2by(index)]
                return pump([c2(index)], [local(sem, 0, rc2.at[index], tmp.at[:, :, all1])], work, sends)
            if kind == J_Z0:

                def work():
                    add_chunks(keep1, pair + (None, z0), tmp, (None, all1), 1)

                return pump([t1z(index)], [local(sem, 0, r1z.at[index], tmp.at[:, all1])], work, [])
            if kind == J_XY1:

                def work():
                    add_chunks(keep2, pair + (None, mx, lo1), tmp, (None, lo1), 1)
                    add_chunks(keep2, pair + (my, None, hi1), tmp, (None, hi1), 1)

                copies = [
                    local(sem, 0, r2ax.at[index], tmp.at[:, lo1]),
                    local(sem, 1, r2by.at[index], tmp.at[:, hi1]),
                ]
                return pump([t2ax(index), t2by(index)], copies, work, [t2ay(index), t2bx(index)])
            if kind == J_XY2:

                def work():
                    r2[pair] = keep2[pair + (my, mx, all1)] + tmp[0, all1]

                copies = [
                    local(sem, 0, r2ay.at[index], tmp.at[0, lo1]),
                    local(sem, 1, r2bx.at[index], tmp.at[0, hi1]),
                ]
                return pump([t2ay(index), t2bx(index)], copies, work, [])
            if kind == J_1A:

                def work():
                    add_chunks(keep1, (index, mx, None, z0, lo1), tmp, (None, lo1), 1)

                return pump([t1ax(index)], [local(sem, 0, r1ax.at[index], tmp.at[:, lo1])], work, [])
            if kind == J_1B:

                def work():
                    add_chunks(keep1, (my, index, None, z0, hi1), tmp, (None, hi1), 1)

                return pump([t1by(index)], [local(sem, 0, r1by.at[index], tmp.at[:, hi1])], work, [])
            if kind == J_1XY2:

                def work():
                    add_chunks(keep1, (my, mx, None, z0, all1), tmp, (None, all1), 1)

                copies = [local(sem, 0, r1ay, tmp.at[:, lo1]), local(sem, 1, r1bx, tmp.at[:, hi1])]
                return pump([t1ay(), t1bx()], copies, work, [t1zz()])
            if kind == J_2Z:

                def work():
                    add_chunks(r2, (None, z0), tmp, (None, all1), 1)

                return pump([t2z()], [local(sem, 0, r2z, tmp.at[:, all1])], work, [t2zz()])
            if kind == J_CO:

                def work():
                    add_chunks(keepo, (0, None, None), tmp_a, (None, None, oab), 2)
                    add_chunks(keepo, (1, None, None), tmp_b, (None, None, oab), 2)

                copies = [
                    local(L_A, 0, rco.at[0], tmp_a.at[:, :, oab]),
                    local(L_B, 0, rco.at[1], tmp_b.at[:, :, oab]),
                ]
                return pump([co()], copies, work, [toax(), toby()])
            if kind == J_O1:

                def work():
                    for i in range(2):
                        add_chunks(keepo, (i, None, mx, oa), tmp, (None, pl.ds(i * so, so)), 1)
                        add_chunks(keepo, (i, my, None, ob), tmp, (None, pl.ds((2 + i) * so, so)), 1)

                copies = [local(sem, i, roax.at[i], tmp.at[:, pl.ds(i * so, so)]) for i in range(2)]
                copies += [local(sem, 2 + i, roby.at[i], tmp.at[:, pl.ds((2 + i) * so, so)]) for i in range(2)]
                return pump([toax(), toby()], copies, work, [toay(), tobx()])
            if kind == J_O2:

                def work():
                    add_chunks(keepo, (None, my, mx, oab), tmp, (None, oab), 1)

                copies = [local(sem, 0, roay, tmp.at[:, oa]), local(sem, 1, robx, tmp.at[:, ob])]
                return pump([toay(), tobx()], copies, work, [toz()])
            if kind == J_OZ:

                def work():
                    add_to(keepo, (z0, my, mx), tmp, (0, oab))

                return pump([toz()], [local(sem, 0, roz, tmp.at[0, oab])], work, [tozz()])
            if kind == J_C0:

                def work():
                    add_chunks(keep2, (index, 0, None, None, all0), tmp_a, (None, None, all0), 2)
                    add_chunks(keep2, (index, 1, None, None, all0), tmp_b, (None, None, all0), 2)

                copies = [
                    local(L_A, 0, rc0.at[index, 0], tmp_a.at[:, :, all0]),
                    local(L_B, 0, rc0.at[index, 1], tmp_b.at[:, :, all0]),
                ]
                sends = [t0ax(index), t0by(index), t0cz(index)]
                return pump([c0(index, f) for f in range(n)], copies, work, sends)
            if kind == J_Q1:

                def work():
                    add_chunks(keep2, (index, None, None, mx, pa), tmp, (None, None, pa), 2)
                    add_chunks(keep2, (index, None, my, None, pb), tmp, (None, None, pb), 2)
                    add_chunks(keep2, (index, z0, None, None, pc), tmp, (None, None, pc), 2)

                copies = [
                    local(sem, i, r.at[index], tmp.at[:, :, p])
                    for i, (r, p) in enumerate(((r0ax, pa), (r0by, pb), (r0cz, pc)))
                ]
                arrivals = [t0ax(index), t0by(index), t0cz(index)]
                return pump(arrivals, copies, work, [t0ay(index), t0bx(index), t0cx(index)])
            if kind == J_Q2:

                def work():
                    add_chunks(keep2, (index, None, my, mx, pab), tmp, (None, pab), 1)
                    add_chunks(keep2, (index, z0, None, mx, pc), tmp, (None, pc), 1)

                copies = [
                    local(sem, i, r.at[index], tmp.at[:, p])
                    for i, (r, p) in enumerate(((r0ay, pa), (r0bx, pb), (r0cx, pc)))
                ]
                return pump([t0ay(index), t0bx(index), t0cx(index)], copies, work, [t0abz(index), t0cy(index)])
            if kind == J_Q3:

                def work():
                    add_to(keep2, (index, z0, my, mx, all0), tmp, (0, all0))

                copies = [local(sem, 0, r0abz.at[index], tmp.at[0, pab]), local(sem, 1, r0cy.at[index], tmp.at[0, pc])]
                return pump([t0abz(index), t0cy(index)], copies, work, [])
            if kind == J_FIN2:

                def work():
                    sum2[...] = r2[z1, z0].astype(F32) + tmp[0, all1].astype(F32)

                return pump([t2zz()], [local(sem, 0, r2zz, tmp.at[0, all1])], work, [])
            if kind == J_FIN1:

                def work():
                    sum1[...] = keep1[my, mx, z1, z0].astype(F32) + tmp[0, all1].astype(F32)

                return pump([t1zz()], [local(sem, 0, r1zz, tmp.at[0, all1])], work, [])
            if kind == J_FINO:

                def work():
                    here = pl.ds(pl.multiple_of(z1 * so, 16), so)
                    sumo[...] = keepo[z0, my, mx, here].astype(F32) + tmp[0, oa].astype(F32)

                return pump([tozz()], [local(sem, 0, rozz, tmp.at[0, oa])], work, [])
            if kind == J_FIN0:

                def work():
                    sum0[...] = keep2[z1, z0, my, mx, all0].astype(F32) + tmp[0, all0].astype(F32)

                return pump([t0zz()], [local(sem, 0, r0zz, tmp.at[0, all0])], work, [])
            if kind == J_SM1:

                def work():
                    sm_b[0] = sm[0] + sm_t[0]

                return pump([smx_send()], [local(L_S, 0, rsm.at[0, 0], sm_t.at[0])], work, [smy_send()])
            if kind == J_SM2:

                def work():
                    smc[0] = sm_b[0] + sm_t[0]

                return pump([smy_send()], [local(L_S, 0, rsm.at[1, 0], sm_t.at[0])], work, [smc_send(0)])
            if kind in (J_MD1, J_MD2):
                step, some = kind - J_MD1, pl.ds(1, clips)
                arrival, sends = (mdx_send, [mdy_send()]) if step == 0 else (mdy_send, [])
                source, result = (sm, sm_b) if step == 0 else (sm_b, small)

                def work():
                    result[some] = source[some] + sm_t[some]

                return pump([arrival()], [local(L_S, 1, rsm.at[step, some], sm_t.at[some])], work, sends)
            step = kind - J_SM3

            def work():
                if step < 2:
                    smc[step + 1] = smc[step] + sm_t[0]
                else:
                    small[0] = smc[step] + sm_t[0]

            sends = [smc_send(step + 1)] if step < 2 else []
            return pump([smc_send(step)], [local(L_S, 0, rsmc.at[step], sm_t.at[0])], work, sends)

        plain_sends = {
            S_1AX: t1ax,
            S_1BY: t1by,
            S_1AY: lambda _: t1ay(),
            S_1BX: lambda _: t1bx(),
            S_2Z: lambda _: t2z(),
            S_0ZZ: lambda _: t0zz(),
            S_SMX: lambda _: smx_send(),
            S_MDX: lambda _: mdx_send(),
            S_OUT: lambda k: row_send(R_OUT, k, out_h),
            S_IN: lambda k: row_send(R_IN, k, in_h),
        }

        def do(point):
            for what, kind, index in SCHEDULE.get(point, ()):
                if what == SEND:
                    plain_sends[kind](index).start()
                else:
                    job(kind, index, TMPS.get((kind, index), TMP_S))[what]()

        def do_in(points, index):
            for k, point in enumerate(points):
                if point in SCHEDULE:
                    pl.when(index == k)(lambda point=point: do(point))

        def weight(slot, src):
            return local(L_W, slot, src, ring.at[slot])

        def fc1_block(f):
            return weight(2 * (f % 2), fc1_h.at[:, pl.ds(pl.multiple_of(f * width, LANES), width)])

        def fc2_block(f):
            return weight(2 * (f % 2) + 1, fc2_h.at[pl.ds(pl.multiple_of(f * width, 16), width)])

        def fc2_block_at(f):
            return local(L_W, f, fc2_h.at[pl.ds(pl.multiple_of(f * width, 16), width)], ring.at[f])

        def qkv_block(i, slot):
            return weight(slot, wqkv_h.at[:, i * width : (i + 1) * width])

        def own_copies(src, dst, name):
            return local(name, 0, src, dst)

        def piece_of(ref, k, c, half):
            return ref[k, c, :, half * 8 : half * 8 + 8, :].astype(F32).reshape(plan.piece, width)

        def rows_at(c, half, k):
            return pl.ds(pl.multiple_of(c * plan.clip_rows + plan.row_of(0, half, k), 8), plan.piece)

        def arrive(name, k, src, dst):
            bit = (None, X, Y, XY)[k]
            return remote(name, k, src.at[:, :, pl.ds(partner[bit][1] * own, own)], dst.at[k], bit)

        barrier = pltpu.get_barrier_semaphore()
        for axis, where in partner:
            pl.semaphore_signal(barrier, inc=1, device_id={axis: where}, device_id_type=MESH)
        mine = pl.ds(frame * own, own)
        own_x = local(L_OWN, 2, x_h.at[:, :, mine], xin.at[0])
        own_x.start()
        for i in range(3):
            qkv_block(i, i).start()
        weight(3, wout_h).start()
        pl.semaphore_wait(barrier, len(partner))
        for k in (3, 1, 2):
            arrive(R_XIN, k, x_h, xin).start()
        sm[...] = jnp.zeros_like(sm)
        for i in range(6):
            values = raw_mod[:, i * width : (i + 1) * width].astype(F32)
            for c in range(clips):
                mod[c, i : i + 1, :] = values[c : c + 1, :]
        parts = [(qv_bias, 0), None, (qv_bias, 1), (out_bias, 0)] + [(fc1_bias, f) for f in range(n)] + [(fc2_bias, 0)]
        for i, part in enumerate(parts):
            if part is None:
                bias[i] = jnp.zeros((1, width), F32)
            else:
                bias[i] = part[0][pl.ds(part[1] * width, width)].astype(F32).reshape(1, width)

        def frame_of(axis):
            slot = lax.broadcasted_iota(jnp.int32, (block, block), axis) // 8
            k, local_frame = slot // fl, slot % fl
            low, high = k % 2, k // 2
            source = low + mx - 2 * low * mx + 2 * (high + my - 2 * high * my)
            return source * fl + local_frame

        lane_patch = lax.broadcasted_iota(jnp.int32, (block, block), 1) % 8
        row_patch = lax.broadcasted_iota(jnp.int32, (block, block), 0) % 8
        row_frame, lane_frame = frame_of(0), frame_of(1)
        for c in range(clips):
            count = counts_ref[c]
            valid[c] = jnp.where(row_frame < count, 1.0, 0.0)
            allowed[c] = jnp.where((lane_patch == row_patch) & (lane_frame < count), 0.0, NEGATIVE)

        def first_half(n1, proj, ctx, scores, lows, probs, n2):
            own_x.wait()

            @pl.loop(0, clips)
            def _(c):
                shift, scale = mod[c, 0:1, :], 1.0 + mod[c, 1:2, :]
                for half in range(plan.halves):
                    for k in range(n):
                        normed, _ = unit(piece_of(xin, k, c, half))
                        n1[rows_at(c, half, k), :] = (normed * scale + shift).astype(BF16)

            own_copies(n1, n1_h, L_N1).start()

            @pl.loop(0, 3)
            def _(i):
                local(L_W, i, fc2_h.at[pl.ds(0, width)], ring.at[i]).wait()
                proj[i] = (mm(n1[...], ring[i]) + bias[i]).astype(BF16)

            fc1_block(0).start()
            fc2_block(0).start()
            own_copies(proj, proj_h, L_PROJ).start()

            @pl.loop(0, blocks)
            def _(b):
                slot = b % 2
                here = pl.ds(pl.multiple_of(b * block, block), block)

                @pl.when(b >= 2)
                def _():
                    local(L_PROBS, slot, probs.at[slot], probs_h.at[b - 2]).wait()

                for h in range(HEADS):
                    _, start, size = head_window(h, plan.head_width)
                    cols = slice(start, start + size)
                    q = proj[0, here, cols] * head_mask(h, plan.head_width)
                    scores[h] = mm_cols(q, proj[1, here, cols]) * factor + allowed[b // plan.halves]
                for h in range(HEADS):
                    score = scores[h]
                    grown = jnp.exp(score - jnp.max(score, axis=-1, keepdims=True))
                    weights = grown * (1.0 / jnp.sum(grown, axis=-1, keepdims=True))
                    probs[slot, h] = weights
                    lows[h] = weights.astype(BF16)

                def head_context(h):
                    _, start, size = head_window(h, plan.head_width)
                    return [mm(lows[h], proj[2, here, start : start + size] * head_mask(h, plan.head_width))]

                def put_context(j, tiles):
                    ctx[here, j * LANES : (j + 1) * LANES] = tiles[0].astype(BF16)

                join_heads(plan.head_width, head_context, put_context)
                local(L_PROBS, slot, probs.at[slot], probs_h.at[b]).start()

            own_copies(ctx, ctx_h, L_CTX).start()
            weight(3, wout_h).wait()
            f1[...] = mm(ctx[...], ring[3]) + bias[3]
            own_copies(f1, att_h, L_ATT).start()

            @pl.loop(0, clips)
            def _(c):
                for half in range(plan.halves):
                    for k in range(n):
                        here = rows_at(c, half, k)
                        middle = piece_of(xin, k, c, half) + mod[c, 2:3, :] * f1[here, :]
                        f2[here, :] = middle
                        normed, _ = unit(middle)
                        n2[here, :] = (normed * (1.0 + mod[c, 4:5, :]) + mod[c, 3:4, :]).astype(BF16)

            own_copies(f2, mid_h, L_MID).start()
            own_copies(n1, n1_h, L_N1).wait()
            own_copies(proj, proj_h, L_PROJ).wait()
            own_copies(ctx, ctx_h, L_CTX).wait()
            for b in (blocks - 2, blocks - 1):
                local(L_PROBS, b % 2, probs.at[b % 2], probs_h.at[b]).wait()

        def mlp(n2, cin, own_cot, n2_turned, dbr, padded, act, act_turned, dh, res):
            padded[...] = jnp.zeros_like(padded)
            n2_turned[...] = n2[...].T
            acc[...] = jnp.zeros_like(acc)
            own_cot.wait()
            for k in (1, 2, 3):
                arrive(R_CIN, k, cot_h, cin).wait_recv()

            @pl.loop(0, clips)
            def _(c):
                for half in range(plan.halves):
                    for k in range(n):
                        here = rows_at(c, half, k)
                        piece = piece_of(cin, k, c, half) * valid[c, k * plan.piece : (k + 1) * plan.piece, 0:1]
                        dres[here, :] = piece.astype(BF16)
                        low = (piece * mod[c, 5:6, :]).astype(BF16)
                        dbr[here, :] = low
                        sm[0, 7:8, :] += jnp.sum(low.astype(F32), axis=0, keepdims=True)

            for f in range(n):
                padded[:, f * pad2 : f * pad2 + width // n] = dbr[:, f * (width // n) : (f + 1) * (width // n)]
            own_copies(f1, att_h, L_ATT).wait()
            own_copies(f2, mid_h, L_MID).wait()

            @pl.loop(0, n)
            def _(f):
                slot = 2 * (f % 2)

                @pl.when(f < n - 1)
                def _():
                    fc1_block(f + 1).start()
                    fc2_block(f + 1).start()

                @pl.when(f == n - 1)
                def _():
                    weight(0, wout_h).start()
                    qkv_block(0, 1).start()

                fc1_block(f).wait()
                f2[...] = mm(n2[...], ring[slot])
                first_bias = bias[4 + f]

                @pl.when(f >= 1)
                def _():
                    local(L_ACT, 0, act, act_h.at[f - 1]).wait()

                @pl.loop(0, rows // half_rows)
                def _(i):
                    here = pl.ds(pl.multiple_of(i * half_rows, half_rows), half_rows)
                    hidden = f2[here, :] + first_bias
                    square = hidden * hidden
                    bent = jnp.tanh(0.7978845608028654 * hidden * (1.0 + 0.044715 * square))
                    act[here, :] = (0.5 * hidden * (1.0 + bent)).astype(BF16)
                    slope = 0.7978845608028654 * (1.0 + 3.0 * 0.044715 * square)
                    f2[here, :] = 0.5 * (1.0 + bent) + 0.5 * hidden * (1.0 - bent * bent) * slope

                local(L_ACT, 0, act, act_h.at[f]).start()

                do_in(P_A, f)

                @pl.when(f >= 1)
                def _():
                    c1(f - 1).wait_send()
                    c2(f - 1).wait_send()

                act_turned[...] = act[...].T
                @pl.loop(0, 2)
                def _(i):
                    lanes = pl.ds(pl.multiple_of(i * 2 * pad2, LANES), 2 * pad2)
                    res[...] = mm(act_turned[...], padded[:, lanes])
                    for mine in (False, True):
                        part = core if mine else 1 - core
                        at = pl.ds(pl.multiple_of(part * span2, 8), span2)
                        for j in range(2):
                            pieces = [res[at, j * pad2 + t * LANES : j * pad2 + (t + 1) * LANES] for t in range(3)]
                            pieces[2] = fold_tile(pieces[2], 4, 32)
                            row = 0
                            for piece in pieces:
                                slab = slice(row, row + piece.shape[0])
                                if mine:
                                    keep2[f // 2, f % 2, i, j, slab, :] = piece.astype(BF16)
                                else:
                                    stage[0, i, j, slab, :] = piece.astype(BF16)
                                row += piece.shape[0]

                c2(f).start()
                do_in(P_B, f)

                fc2_block(f).wait()
                dh[...] = (mm_cols(dbr[...], ring[slot + 1]) * f2[...]).astype(BF16)
                sm[0, pl.ds(3 + f, 1), :] = jnp.sum(dh[...].astype(F32), axis=0, keepdims=True)

                do_in(P_C, f)

                for first, tiles in ((0, 5), (5, 4)):
                    lanes = slice(first * LANES, (first + tiles) * LANES)
                    res[:, : tiles * LANES] = mm(n2_turned[...], dh[:, lanes])
                    for mine in (False, True):
                        part = core if mine else 1 - core
                        for i in range(2):
                            for j in range(2):
                                at = pl.ds(pl.multiple_of((4 * i + 2 * j + part) * span1, 8), span1)
                                for t in range(tiles):
                                    slab = slice((first + t) * span1, (first + t + 1) * span1)
                                    values = res[at, t * LANES : (t + 1) * LANES].astype(BF16)
                                    if mine:
                                        keep1[f // 2, f % 2, i, j, slab, :] = values
                                    else:
                                        stage[1, i, j, slab, :] = values
                c1(f).start()

                do_in(P_D, f)
                acc[...] += mm_cols(dh[...], ring[slot])
                do_in(P_E, f)

            local(L_ACT, 0, act, act_h.at[n - 1]).wait()

        def two_halves(n2):
            own_cot = local(L_OWN, 3, cot_h.at[:, :, mine], cin.at[0])
            own_cot.start()
            for k in (1, 2, 3):
                arrive(R_XIN, k, x_h, xin).wait_recv()
            for k in (3, 1, 2):
                arrive(R_CIN, k, cot_h, cin).start()
            pl.run_scoped(
                functools.partial(first_half, n2=n2),
                pltpu.VMEM((rows, width), BF16),
                pltpu.VMEM((3, rows, width), BF16),
                pltpu.VMEM((rows, width), BF16),
                pltpu.VMEM((HEADS, block, block), F32),
                pltpu.VMEM((HEADS, block, block), BF16),
                pltpu.VMEM((2, HEADS, block, block), F32),
            )
            pl.run_scoped(
                functools.partial(mlp, n2, cin, own_cot),
                pltpu.VMEM((width, rows), BF16),
                pltpu.VMEM((rows, width), BF16),
                pltpu.VMEM((rows, n * pad2), BF16),
                pltpu.VMEM((rows, width), BF16),
                pltpu.VMEM((width, rows), BF16),
                pltpu.VMEM((rows, width), BF16),
                pltpu.VMEM((width, 2 * pad2), F32),
            )

        pl.run_scoped(two_halves, pltpu.VMEM((rows, width), BF16))

        def rest(datt, proj):
            own_copies(mid_h, f2, L_MID).start()
            own_copies(proj_h, proj, L_PROJ).start()
            qkv_block(1, 3).start()
            own_copies(ctx_h, ring.at[2, :rows], L_CTX).start()

            def attend(dctx, probs, scores, lows):
                def middle(att):
                    own_copies(att_h, att, L_ATT).start()
                    own_copies(mid_h, f2, L_MID).wait()
                    own_copies(att_h, att, L_ATT).wait()

                    @pl.loop(0, rows // half_rows)
                    def _(i):
                        here = pl.ds(pl.multiple_of(i * half_rows, half_rows), half_rows)
                        c = i // parts_per_clip
                        normed, inverse = unit_rows(f2, here)
                        grad = acc[here, :]
                        sm[1 + c, 3:4, :] += jnp.sum(grad, axis=0, keepdims=True)
                        sm[1 + c, 4:5, :] += jnp.sum(grad * normed, axis=0, keepdims=True)
                        d_middle = dres[here, :].astype(F32) + unit_back(normed, inverse, grad * (1.0 + mod[c, 4:5, :]))
                        acc[here, :] = d_middle
                        sm[1 + c, 2:3, :] += jnp.sum(d_middle * att[here, :], axis=0, keepdims=True)
                        low = (d_middle * mod[c, 2:3, :]).astype(BF16)
                        datt[here, :] = low
                        sm[0, 2:3, :] += jnp.sum(low.astype(F32), axis=0, keepdims=True)

                pl.run_scoped(middle, pltpu.VMEM((rows, width), F32))
                do(P_M1)
                local(L_PROBS, 0, probs_h.at[0], probs.at[0]).start()

                c1(3).wait_send()
                c2(3).wait_send()

                def out_grad(right_o, res):
                    wide = width // n
                    right_o[...] = jnp.zeros_like(right_o)
                    for f in range(n):
                        right_o[f, :, :wide] = datt[:, f * wide : (f + 1) * wide]
                    own_copies(ctx_h, ring.at[2, :rows], L_CTX).wait()
                    turned = ring[2, :rows, :].T
                    ring[2, :, rows : 2 * rows] = turned

                    @pl.loop(0, n)
                    def _(f):
                        res[...] = mm(ring[2, :, rows : 2 * rows], right_o[f])
                        for mine in (False, True):
                            part = core if mine else 1 - core
                            for i in range(2):
                                for j in range(2):
                                    at = pl.ds(pl.multiple_of((4 * i + 2 * j + part) * span1, 8), span1)
                                    pieces = [res[at, t * LANES : (t + 1) * LANES] for t in range(3)]
                                    pieces[2] = fold_tile(pieces[2], 3, 32)
                                    row = i * so
                                    for piece in pieces:
                                        slab = slice(row, row + piece.shape[0])
                                        if mine:
                                            keepo[j, f // 2, f % 2, slab, :] = piece.astype(BF16)
                                        else:
                                            stage[j, f // 2, f % 2, slab, :] = piece.astype(BF16)
                                        row += piece.shape[0]

                pl.run_scoped(
                    out_grad, pltpu.VMEM((n, rows, pad2), BF16), pltpu.VMEM((width, pad2), F32)
                )
                co().start()
                do(P_WO)
                weight(0, wout_h).wait()
                dctx[...] = mm_cols(datt[...], ring[0]).astype(BF16)
                qkv_block(2, 0).start()
                do(P_DC)
                own_copies(proj_h, proj, L_PROJ).wait()

                @pl.loop(0, blocks)
                def _(b):
                    slot = b % 2
                    here = pl.ds(pl.multiple_of(b * block, block), block)

                    @pl.when(b < blocks - 1)
                    def _():
                        local(L_PROBS, 1 - slot, probs_h.at[b + 1], probs.at[1 - slot]).start()

                    local(L_PROBS, slot, probs_h.at[b], probs.at[slot]).wait()
                    for h in range(HEADS):
                        _, start, size = head_window(h, plan.head_width)
                        cols = slice(start, start + size)
                        scores[h] = mm_cols(dctx[here, cols] * head_mask(h, plan.head_width), proj[2, here, cols])
                    for h in range(HEADS):
                        weights = probs[slot, h]
                        mixed = weights * scores[h]
                        d_score = mixed - weights * jnp.sum(mixed, axis=-1, keepdims=True)
                        lows[0, h] = d_score.astype(BF16)
                        lows[1, h] = weights.astype(BF16)

                    def head_grads(h):
                        _, start, size = head_window(h, plan.head_width)
                        keep = head_mask(h, plan.head_width)
                        cols = slice(start, start + size)
                        return [
                            mm(lows[0, h], proj[1, here, cols] * keep),
                            mm_rows(lows[0, h], proj[0, here, cols] * keep),
                            mm_rows(lows[1, h], dctx[here, cols] * keep),
                        ]

                    def put_grads(j, tiles):
                        lanes = slice(j * LANES, (j + 1) * LANES)
                        for part in range(3):
                            values = tiles[part] if part == 2 else tiles[part] * factor
                            low = values.astype(BF16)
                            proj[part, here, lanes] = low
                            if part != 1:
                                at = part // 2
                                sm[0, at : at + 1, lanes] += jnp.sum(low.astype(F32), axis=0, keepdims=True)

                    join_heads(plan.head_width, head_grads, put_grads)

                    do_in(P_AB, b)

            pl.run_scoped(
                attend,
                pltpu.VMEM((rows, width), BF16),
                pltpu.VMEM((2, HEADS, block, block), F32),
                pltpu.VMEM((HEADS, block, block), F32),
                pltpu.VMEM((2, HEADS, block, block), BF16),
            )

            def weight_grads(right_q, left, res):
                own_copies(n1_h, left, L_N1).start()
                right_q[...] = jnp.zeros_like(right_q)
                for f in range(n):
                    low, high = f * wq, (f + 1) * wq
                    for part in range(3):
                        a, b = max(low, part * width), min(high, (part + 1) * width)
                        if a < b:
                            right_q[f, :, a - low : b - low] = proj[part, :, a - part * width : b - part * width]
                own_copies(n1_h, left, L_N1).wait()
                ring[2, :, :rows] = left[...].T
                do(P_PK)
                for z in range(4):
                    t2ax(z).wait_send()
                    t2by(z).wait_send()
                    t2ay(z).wait_send()
                    t2bx(z).wait_send()
                co().wait_send()

                @pl.loop(0, 2 * n)
                def _(step):
                    j, f = step // n, step % n
                    lines = pl.ds(pl.multiple_of(j * 4 * span1, 16), 4 * span1)

                    @pl.when(j == 1)
                    def _():
                        c0(0, f).wait_send()

                    res[...] = mm(ring[2, lines, :rows], right_q[f])
                    for mine in (False, True):
                        part = core if mine else 1 - core
                        for i in range(2):
                            at = pl.ds(pl.multiple_of((2 * i + part) * span1, 8), span1)
                            for t in range(padq // LANES):
                                slab = slice(t * span1, (t + 1) * span1)
                                piece = res[at, t * LANES : (t + 1) * LANES].astype(BF16)
                                if mine:
                                    keep2[j, i, f // 2, f % 2, slab, :] = piece
                                else:
                                    stage[i, f // 2, f % 2, slab, :] = piece
                    c0(j, f).start()
                    do_in(P_WQ, step)

            pl.run_scoped(
                weight_grads,
                pltpu.VMEM((n, rows, padq), BF16),
                pltpu.VMEM((rows, width), BF16),
                pltpu.VMEM((4 * span1, padq), F32),
            )

            f1[...] = jnp.zeros_like(f1)

            @pl.loop(0, 3)
            def _(i):
                slot = (2 * i + 1) % 5
                local(L_W, slot, fc2_h.at[pl.ds(0, width)], ring.at[slot]).wait()
                f1[...] += mm_cols(proj[i], ring[slot])
                do_in(P_IN, i)

            for f in range(n):
                weight(f, fc2_h.at[pl.ds(f * width, width)]).start()

            @pl.loop(0, clips)
            def _(c):
                for half in range(plan.halves):
                    for k in range(n):
                        here = rows_at(c, half, k)
                        normed, inverse = unit(piece_of(xin, k, c, half))
                        grad = f1[here, :]
                        sm[1 + c, 0:1, :] += jnp.sum(grad, axis=0, keepdims=True)
                        sm[1 + c, 1:2, :] += jnp.sum(grad * normed, axis=0, keepdims=True)
                        total = acc[here, :] + unit_back(normed, inverse, grad * (1.0 + mod[c, 1:2, :]))
                        rows_out[k, c, :, half * 8 : half * 8 + 8, :] = total.reshape(fl, 8, width).astype(BF16)

            row_own(1, rows_out, in_h).start()
            do(P_INE)

            def branch(acts):
                for f in range(n):
                    local(L_ACTS, f, act_h.at[f], acts.at[f]).start()
                f1[...] = jnp.zeros_like(f1)

                @pl.loop(0, n)
                def _(f):
                    local(L_ACTS, f, act_h.at[f], acts.at[f]).wait()
                    fc2_block_at(f).wait()
                    f1[...] += mm(acts[f], ring[f])
                    do_in(P_G, f)

            pl.run_scoped(branch, pltpu.VMEM((n, rows, width), BF16))

            @pl.loop(0, clips)
            def _(c):
                for half in range(plan.halves):
                    for k in range(n):
                        here = rows_at(c, half, k)
                        value = f1[here, :] + bias[8]
                        sm[1 + c, 5:6, :] += jnp.sum(dres[here, :].astype(F32) * value, axis=0, keepdims=True)
                        total = valid[c, k * plan.piece : (k + 1) * plan.piece, 0:1] * (
                            f2[here, :] + mod[c, 5:6, :] * value
                        )
                        cin[k, c, :, half * 8 : half * 8 + 8, :] = total.reshape(fl, 8, width).astype(BF16)

            row_own(0, cin, out_h).start()
            do(P_O)

            for k in (1, 2, 3):
                arrive(R_XIN, k, x_h, xin).wait_send()
                arrive(R_CIN, k, cot_h, cin).wait_send()
            row_own(1, rows_out, in_h).wait()
            row_own(0, cin, out_h).wait()
            for k in (1, 2, 3):
                row_send(R_OUT, k, out_h, True).wait_recv()
                row_send(R_IN, k, in_h, True).wait_recv()
                row_send(R_IN, k, in_h).wait_send()
                row_send(R_OUT, k, out_h).wait_send()
            for transfer in (smx_send, smy_send, mdx_send, mdy_send):
                transfer().wait_send()
            for i in range(3):
                smc_send(i).wait_send()
            for f in range(n):
                t1z(f).wait_send()
                c0(1, f).wait_send()
            for j in range(2):
                for transfer in (t1ax, t1by, t0ax, t0by, t0cz, t0ay, t0bx, t0cx, t0abz, t0cy):
                    transfer(j).wait_send()
            for transfer in (t2z, t2zz, t1ay, t1bx, t1zz, toax, toby, toay, tobx, toz, tozz, t0zz):
                transfer().wait_send()

        pl.run_scoped(rest, pltpu.VMEM((rows, width), BF16), pltpu.VMEM((3, rows, width), BF16))

    lanes = LANES
    image = shape((clips, fl, plan.patches, width), BF16)
    arriving = [
        (4, 2, 2, s1), (4, 2, 2, s1), (2, 2, 2, 2, s0), (2, 2, 2, 2 * so),
        (4, 2, a1), (4, 2, s1 - a1), (4, a1), (4, s1 - a1), (2, s1), (s1,),
        (4, 2, s1), (2, 2, a1), (2, 2, s1 - a1), (2, a1), (2, s1 - a1), (s1,),
        (2, 2, so), (2, 2, so), (2, so), (2, so), (2 * so,), (so,),
        (2, 2, 2, a0), (2, 2, 2, a0), (2, 2, 2, a0), (2, 2, a0), (2, 2, a0), (2, 2, a0), (2, 2 * a0), (2, a0), (s0,),
    ]
    vmem = pl.BlockSpec(memory_space=pltpu.VMEM)
    smalls = (1 + clips, 8, width)
    out_shape = (
        [image, image, shape((s1, lanes), F32), shape((s1, lanes), F32), shape((s0, lanes), F32), shape((so, lanes), F32), shape(smalls, F32)]
        + [shape(dims + (lanes,), BF16) for dims in arriving]
        + [shape((2,) + smalls, F32), shape((3, 8, width), F32)]
        + [shape((rows, width), BF16)] * 2
        + [shape((3, rows, width), BF16), shape((blocks, HEADS, block, block), F32)]
        + [shape((rows, width), F32)] * 2
        + [shape((n, rows, width), BF16)]
    )
    out_specs = [ANY, ANY] + [vmem] * 5 + [ANY] * (len(arriving) + 9)
    scratch = [
        pltpu.VMEM((2, 2, 2, 2, s1, lanes), BF16),
        pltpu.VMEM((2, 2, 2, 2, s1, lanes), BF16),
        pltpu.VMEM((2, 2, 2, 2 * so, lanes), BF16),
        pltpu.VMEM((2, 2, s1, lanes), BF16),
        pltpu.VMEM((2, 2, 2, s1, lanes), BF16),
        pltpu.VMEM((2, 2, s1, lanes), BF16),
        pltpu.VMEM((2, 2, s1, lanes), BF16),
        pltpu.VMEM((2, 4 * so, lanes), BF16),
        pltpu.VMEM((2, 4 * so, lanes), BF16),
        pltpu.VMEM((rows, width), BF16),
        pltpu.VMEM((rows, width), F32),
        pltpu.VMEM((rows, width), F32),
        pltpu.VMEM((rows, width), F32),
        pltpu.VMEM((4, width, width), BF16),
        pltpu.VMEM((n, clips, fl, own, width), BF16),
        pltpu.VMEM(smalls, F32),
        pltpu.VMEM(smalls, F32),
        pltpu.VMEM(smalls, F32),
        pltpu.VMEM((3, 8, width), F32),
        pltpu.VMEM((n, clips, fl, own, width), BF16),
        pltpu.VMEM((n, clips, fl, own, width), BF16),
        pltpu.VMEM((clips, 8, width), F32),
        pltpu.VMEM((9, 1, width), F32),
        pltpu.VMEM((clips, block, block), F32),
        pltpu.VMEM((clips, block, block), F32),
        pltpu.SemaphoreType.DMA((sum(REMOTE_SIZES),)),
        pltpu.SemaphoreType.DMA((sum(REMOTE_SIZES),)),
        pltpu.SemaphoreType.DMA((sum(LOCAL_SIZES),)),
    ]
    result = pl.pallas_call(
        body,
        in_specs=[ANY] * 6 + [vmem, pl.BlockSpec(memory_space=pltpu.SMEM)] + [vmem] * 4,
        out_specs=out_specs,
        out_shape=out_shape,
        scratch_shapes=scratch,
        compiler_params=pltpu.CompilerParams(
            vmem_limit_bytes=VMEM_LIMIT, collective_id=0, has_side_effects=True
        ),
        cost_estimate=cost(45e9, 200e6),
        name="layer",
    )(x, cotangent, qkv_weight, out_weight, fc1_weight, fc2_weight, modulation, counts, *biases)
    return result[:7]


def close(plan, images, small, sums, layouts):
    n, width, clips = plan.frame_axis, plan.width, plan.clips
    m = len(images)

    def body(*refs):
        refs = list(refs)

        def take(count):
            got = refs[:count]
            del refs[:count]
            return got

        image_in, (vectors,), sums_in = take(m), take(1), take(len(sums))
        image_out, outs_h = take(m), take(len(layouts))
        d_mod, d_qv, d_out, d_fc1, d_fc2 = take(5)
        ins, outs, (turn, held, sems) = take(len(sums)), take(len(layouts)), take(3)
        arrive = [pltpu.make_async_copy(sums_in[i], ins[i], sems.at[i]) for i in range(len(sums))]
        arrive += [pltpu.make_async_copy(image_in[i], held.at[i], sems.at[len(sums) + i]) for i in range(m)]
        there = len(arrive)
        leave = [pltpu.make_async_copy(outs[i], outs_h[i], sems.at[there + i]) for i in range(len(layouts))]
        leave += [pltpu.make_async_copy(held.at[i], image_out[i], sems.at[there + len(layouts) + i]) for i in range(m)]
        for copy in arrive:
            copy.start()
        frame = lax.axis_index("frame")

        def cut(first, k, size):
            low, high, pieces = k * size, (k + 1) * size, []
            while low < high:
                row, at = low // width, low % width
                end = min(width, at + high - low)
                pieces.append(vectors[first[0], first[1] + row : first[1] + row + 1, at:end])
                low += end - at
            return pieces[0] if len(pieces) == 1 else jnp.concatenate(pieces, axis=1)

        for k in range(n):

            @pl.when(frame == k)
            def _(k=k):
                for c in range(clips):
                    d_mod[c : c + 1, :] = cut((1 + c, 0), k, 6 * width // n)
                d_qv[...] = cut((0, 0), k, 2 * width // n).reshape(2 * width // n)
                d_out[...] = cut((0, 2), k, width // n).reshape(width // n)
                d_fc1[...] = cut((0, 3), k, width).reshape(width)
                d_fc2[...] = cut((0, 7), k, width // n).reshape(width // n)

        for at, (which, first, span, tiles, used, folds, turned) in enumerate(layouts):
            ref, out = ins[which], outs[at]
            arrive[which].wait()
            to = turn if turned else out
            for j in range(tiles):
                to[:, j * LANES : (j + 1) * LANES] = ref[first + j * span : first + (j + 1) * span, :]
            if used:
                tile = ref[first + tiles * span : first + tiles * span + span // folds, :]
                for g in range(folds):
                    moved = tile if g == 0 else pltpu.roll(tile, LANES - g * used, 1)
                    here = slice(g * (span // folds), (g + 1) * (span // folds))
                    to[here, tiles * LANES : tiles * LANES + used] = moved[:, :used]
            if turned:
                out[...] = turn[...].T
            leave[at].start()
        for i in range(m):
            arrive[len(sums) + i].wait()
            leave[len(layouts) + i].start()
        for copy in leave:
            copy.wait()

    dims = [(span, tiles * LANES + used) for _, _, span, tiles, used, _, _ in layouts]
    grads = [shape(d[::-1] if layout[-1] else d, F32) for d, layout in zip(dims, layouts)]
    sizes = (2 * width // n, width // n, width, width // n)
    vectors = [shape((clips, 6 * width // n), F32)] + [shape((size,), F32) for size in sizes]
    made = grads + vectors
    return pl.pallas_call(
        body,
        grid=(1,),
        in_specs=[ANY] * m + [whole(small.shape)] + [ANY] * len(sums),
        out_specs=[ANY] * (m + len(grads)) + [whole(s.shape) for s in vectors],
        out_shape=[shape(image.shape, image.dtype) for image in images] + made,
        scratch_shapes=[pltpu.VMEM(s.shape, s.dtype) for s in list(sums) + grads]
        + [
            pltpu.VMEM(dims[0], F32),
            pltpu.VMEM((m,) + images[0].shape, images[0].dtype),
            pltpu.SemaphoreType.DMA((2 * m + len(sums) + len(layouts),)),
        ],
        compiler_params=params(),
        cost_estimate=cost(0, 14e6),
        name="close",
    )(*images, small, *sums)


def fast_layer(
    mesh,
    block_input,
    modulation,
    frame_counts,
    qkv_weight,
    qv_bias,
    out_weight,
    out_bias,
    fc1_weight,
    fc1_bias,
    fc2_weight,
    fc2_bias,
    out_cotangent,
):
    plan = Plan(mesh, block_input.shape, qkv_weight.shape, fc1_weight.shape)
    n, width = plan.frame_axis, plan.width
    biases = (qv_bias, out_bias, fc1_bias, fc2_bias)
    block_output, input_grad, sum2, sum1, sum0, sumo, small = whole_layer(
        plan, block_input, out_cotangent, modulation, frame_counts, biases, qkv_weight, out_weight, fc1_weight, fc2_weight
    )
    span2, span1 = plan.ff // plan.clip_axis, width // plan.clip_axis
    (block_output, input_grad, fc2_turned, fc1_out, qkv_out, out_out, d_modulation, d_qv, d_out, d_fc1, d_fc2) = close(
        plan,
        (block_output, input_grad),
        small,
        (sum2, sum1, sum0, sumo),
        (
            (0, 0, span2, 2, 32, 4, True),
            (1, 0, span1, 9, 0, 1, False),
            (2, 0, span1, 6, 96, 1, False),
            (3, 0, span1, 2, 32, 3, False),
        ),
    )
    return (
        block_output,
        input_grad,
        d_modulation,
        qkv_out,
        d_qv,
        out_out,
        d_out,
        fc1_out,
        d_fc1,
        fc2_turned.T,
        d_fc2,
    )


def solution(mesh):
    placed = (
        P("clip", "frame", None, None),
        P("clip", None),
        P("clip"),
        P(),
        P(),
        P(),
        P(),
        P(),
        P(),
        P(),
        P(),
        P("clip", "frame", None, None),
    )
    def layer(*arrays):
        if fits(mesh, arrays[0].shape, arrays[3].shape, arrays[7].shape):
            return fast_layer(mesh, *arrays)
        return on_device(*arrays)

    return jax.shard_map(
        layer,
        mesh=mesh,
        in_specs=placed,
        out_specs=(
            P("clip", "frame", None, None),
            P("clip", "frame", None, None),
            P("clip", "frame"),
            P("clip", "frame"),
            P("frame"),
            P("clip", "frame"),
            P("frame"),
            P("clip", "frame"),
            P("frame"),
            P("clip", "frame"),
            P("frame"),
        ),
        check_vma=False,
    )
```

profile of v0, /device:TPU:0, one launch (start us, length us, event | category | flops | bytes accessed | tf_op | source)
XLA Modules:
  0.0 221.1 jit_solution(14455544385552583104)
XLA Ops:
  0.6 215.1 %layer.1 = (bf16[2,4,64,1152]{3,2,1,0:T(8,128)(2,1)}, bf16[2,4,64,1152]{3,2,1,0:T(8,128)(2,1)}, f32[1296,128]{1,0:T(8,128)}, f32[1296,128]{1,0:T(8,128)}, f32[10...) custom-call(bf16[2,4,64,1152]{3,2,1,0:T(8,128)(2,1)} %refs_0_.1, ...), custom_call_target="tpu_custom_call" | custom-call | flops 44999999488 | bytes 200000000 | tf_op jit(solution)/shard_map/layer/pallas_call | solution.py:1672
  215.7 5.2 %close.1 = (bf16[2,4,64,1152]{3,2,1,0:T(8,128)(2,1)}, bf16[2,4,64,1152]{3,2,1,0:T(8,128)(2,1)}, f32[288,576]{1,0:T(8,128)}, f32[144,1152]{1,0:T(8,128)}, f32[144...) custom-call(bf16[2,4,64,1152]{3,2,1,0:T(8,128)(2,1)} %get-tuple-elem, ...), custom_call_target="tpu_custom_call" | custom-call | bytes 14000000 | tf_op jit(solution)/shard_map/close/pallas_call | solution.py:1758
where the time goes:
time: 222 us; the launch traced here: 221 us
  Pallas kernels  220 us (99%)
    pallas_call x1, Pallas kernels, whole_layer(): pl.pallas_call(body, in_specs=[ANY] * 6 + [vmem, pl.BlockSpec(memory_spac...  215 us
    pallas_call x1, Pallas kernels, close(): pl.pallas_call(body, grid=(1,), in_specs=[ANY] * m + [whole(small.shape)]...  5.2 us

commit v1 on v0

--- a/solution.py
+++ b/solution.py
@@ -642,7 +642,7 @@
     pad2, padq, wq = 384, 896, 3 * width // n
     blocks, block = plan.blocks, plan.block
     factor = plan.head_width ** (-0.5)
-    half_rows = 64
+    half_rows = 128
     parts_per_clip = plan.clip_rows // half_rows
 
     def body(*refs):

time: 222 us -> 221 us (level)
  no operation moved by 1% of the time
where the time goes in v1:
time: 221 us; the launch traced here: 220 us
  Pallas kernels  219 us (99%)
    pallas_call x1, Pallas kernels, whole_layer(): pl.pallas_call(body, in_specs=[ANY] * 6 + [vmem, pl.BlockSpec(memory_spac...  214 us
    pallas_call x1, Pallas kernels, close(): pl.pallas_call(body, grid=(1,), in_specs=[ANY] * m + [whole(small.shape)]...  5.2 us

profile of v1, /device:TPU:0, one launch (start us, length us, event | category | flops | bytes accessed | tf_op | source)
XLA Modules:
  0.0 220.3 jit_solution(1324237986549023683)
XLA Ops:
  0.6 214.2 %layer.1 = (bf16[2,4,64,1152]{3,2,1,0:T(8,128)(2,1)}, bf16[2,4,64,1152]{3,2,1,0:T(8,128)(2,1)}, f32[1296,128]{1,0:T(8,128)}, f32[1296,128]{1,0:T(8,128)}, f32[10...) custom-call(bf16[2,4,64,1152]{3,2,1,0:T(8,128)(2,1)} %refs_0_.1, ...), custom_call_target="tpu_custom_call" | custom-call | flops 44999999488 | bytes 200000000 | tf_op jit(solution)/shard_map/layer/pallas_call | solution.py:1672
  214.9 5.2 %close.1 = (bf16[2,4,64,1152]{3,2,1,0:T(8,128)(2,1)}, bf16[2,4,64,1152]{3,2,1,0:T(8,128)(2,1)}, f32[288,576]{1,0:T(8,128)}, f32[144,1152]{1,0:T(8,128)}, f32[144...) custom-call(bf16[2,4,64,1152]{3,2,1,0:T(8,128)(2,1)} %get-tuple-elem, ...), custom_call_target="tpu_custom_call" | custom-call | bytes 14000000 | tf_op jit(solution)/shard_map/close/pallas_call | solution.py:1758
